TPU v7x, 32 devices: a whole 2x2x4 slice. The times are simulated.
32 devices in a mesh: batch: 8 (over z, y), head: 4 (over x, core).
Axes of the slice: x: 2, y: 2, z: 4, core: 2. Of those that a mesh axis runs over, the one named last changes fastest.
Arguments:
- tokens: bfloat16 [16384, 768], P(('batch', 'head')), may hold values from -6 to 6
- cotangent: bfloat16 [16384, 768], P(('batch', 'head')), may hold values from -6 to 6
- lengths: int32 [32], P('batch'), may hold values from 16 to 512, as said below
- labels: int32 [32], P('batch'), may hold values from 0 to 2
- w_qkv: bfloat16 [768, 2304], replicated, may hold values from -0.21875 to 0.21875
- w_out: bfloat16 [768, 768], replicated, may hold values from -0.875 to 0.875
- w_up: bfloat16 [768, 3072], replicated, may hold values from -0.21875 to 0.21875
- w_down: bfloat16 [3072, 768], replicated, may hold values from -0.109375 to 0.109375
- w_pool: bfloat16 [768, 768], replicated, may hold values from -0.21875 to 0.21875
- w_class: bfloat16 [3, 768], replicated, may hold values from -0.625 to 0.625
- biases: float32 [7, 768], replicated, may hold values from -3 to 3
- norm_gains: float32 [2, 768], replicated, may hold values from 0.25 to 1.75
- bias_up: float32 [3072], replicated, may hold values from -3 to 3
Outputs:
- out: bfloat16 [16384, 768], P(('batch', 'head'))
- grad_tokens: bfloat16 [16384, 768], P(('batch', 'head'))
- losses: float32 [32], P(('batch', 'head'))
- g_qkv: float32 [768, 2304], P(None, ('batch', 'head'))
- g_out: float32 [768, 768], P(None, ('batch', 'head'))
- g_up: float32 [768, 3072], P(None, ('batch', 'head'))
- g_down: float32 [3072, 768], P(None, ('batch', 'head'))
- g_pool: float32 [768, 768], P(None, ('batch', 'head'))
- g_class: float32 [3, 768], P(None, ('batch', 'head'))
- g_biases: float32 [6, 768], P(None, ('batch', 'head'))
- g_gains: float32 [2, 768], P(None, ('batch', 'head'))
- g_bias_up: float32 [3072], P(('batch', 'head'))
- g_pool_bias: float32 [768], P(('batch', 'head'))
Inputs may be any that keep to these rules, and one draw needn't show every extreme that they name: `lengths`: some sequence has exactly 512 and some exactly 16 positions.
All inputs are finite; a program needn't handle non-finite values.
Results may differ from a plain program's by a relative error of at most 0.014.
Values may be sent and summed in bfloat16 or wider, within the bound.
A program may use at most 192 MiB of HBM per device.

v0:
```python
import jax
import jax.numpy as jnp
from jax import lax
from jax.sharding import PartitionSpec as P

D = 768
HEADS = 12
HEAD_DIM = 64
CLASSES = 3
SLOT = 512


def layer_norm(hidden, gain, shift):
    center = hidden - jnp.mean(hidden, axis=-1, keepdims=True)
    spread = jnp.mean(center * center, axis=-1, keepdims=True)
    return center * lax.rsqrt(spread + 1e-12) * gain + shift


def exact_gelu(hidden):
    return jax.nn.gelu(hidden, approximate=False)


def inner(left, right):
    return lax.dot_general(
        left, right, (((0,), (0,)), ((), ())), preferred_element_type=jnp.float32
    )


def against(left, right):
    return lax.dot_general(
        left, right, (((1,), (1,)), ((), ())), preferred_element_type=jnp.float32
    )


def exact(left, right):
    return jnp.dot(left, right, precision=lax.Precision.HIGHEST, preferred_element_type=jnp.float32)


def masked_scores(queries, keys_all, length):
    scores = jnp.einsum(
        "qhd,khd->hqk", queries, keys_all, preferred_element_type=jnp.float32
    ) * HEAD_DIM ** (-0.5)
    allowed = jnp.arange(SLOT) < length
    return jnp.where(allowed[None, None, :], scores, -1e30)


def attend_forward(seq_item):
    packed, length = seq_item
    queries = packed[:, 0]
    keys_all = packed[:, 1]
    values = packed[:, 2]
    scores = masked_scores(queries, keys_all, length)
    row_max = jnp.max(scores, axis=-1, keepdims=True)
    exp_sum = jnp.sum(jnp.exp(scores - row_max), axis=-1, keepdims=True)
    log_total = row_max + jnp.log(exp_sum)
    weights = jnp.exp(scores - log_total).astype(jnp.bfloat16)
    context = jnp.einsum("hqk,khd->qhd", weights, values, preferred_element_type=jnp.float32)
    return (context.astype(jnp.bfloat16), log_total)


def attend_backward(seq_item):
    packed, log_total, d_context, length = seq_item
    queries = packed[:, 0]
    keys_all = packed[:, 1]
    values = packed[:, 2]
    scores = masked_scores(queries, keys_all, length)
    weights = jnp.exp(scores - log_total)
    weights_low = weights.astype(jnp.bfloat16)
    d_weights = jnp.einsum("qhd,khd->hqk", d_context, values, preferred_element_type=jnp.float32)
    d_values = jnp.einsum(
        "hqk,qhd->khd", weights_low, d_context, preferred_element_type=jnp.float32
    )
    row_dot = jnp.sum(weights * d_weights, axis=-1, keepdims=True)
    d_scores = (weights * (d_weights - row_dot)).astype(jnp.bfloat16)
    d_queries = jnp.einsum(
        "hqk,khd->qhd", d_scores, keys_all, preferred_element_type=jnp.float32
    ) * HEAD_DIM ** (-0.5)
    d_keys = jnp.einsum(
        "hqk,qhd->khd", d_scores, queries, preferred_element_type=jnp.float32
    ) * HEAD_DIM ** (-0.5)
    return jnp.stack([d_queries, d_keys, d_values], axis=1).astype(jnp.bfloat16)


def per_device(
    tokens,
    cotangent,
    lengths,
    labels,
    w_qkv,
    w_out,
    w_up,
    w_down,
    w_pool,
    w_class,
    biases,
    norm_gains,
    bias_up,
):
    head_parts = lax.axis_size("head")
    head_rank = lax.axis_index("head")
    tok_rows = tokens.shape[0]
    own_seqs = tok_rows // SLOT
    local_heads = HEADS // head_parts
    slice_width = D // head_parts
    own_lengths = lax.dynamic_slice_in_dim(lengths, head_rank * own_seqs, own_seqs)
    own_labels = lax.dynamic_slice_in_dim(labels, head_rank * own_seqs, own_seqs)
    slot_live = (
        (jnp.arange(SLOT)[None, :] < own_lengths[:, None]).reshape(tok_rows).astype(jnp.float32)
    )
    zeros_key = jnp.zeros((D,), jnp.float32)
    packed = jnp.dot(tokens, w_qkv, preferred_element_type=jnp.float32) + jnp.concatenate(
        [biases[0], zeros_key, biases[1]]
    )
    packed_low = packed.astype(jnp.bfloat16)
    head_view = lax.all_to_all(
        packed_low.reshape(tok_rows, 3, head_parts, slice_width),
        "head",
        split_axis=2,
        concat_axis=0,
        tiled=True,
    )
    seq_view = head_view.reshape(head_parts * own_seqs, SLOT, 3, local_heads, HEAD_DIM)
    context, log_total = lax.map(attend_forward, (seq_view, lengths))
    context_back = lax.all_to_all(
        context.reshape(head_parts * tok_rows, 1, slice_width),
        "head",
        split_axis=0,
        concat_axis=1,
        tiled=True,
    )
    context_tok = context_back.reshape(tok_rows, D)
    attn = jnp.dot(context_tok, w_out, preferred_element_type=jnp.float32) + biases[2]
    first_sum = tokens.astype(jnp.float32) + attn
    norm_one, first_pull = jax.vjp(layer_norm, first_sum, norm_gains[0], biases[3])
    norm_low = norm_one.astype(jnp.bfloat16)
    hidden_up = jnp.dot(norm_low, w_up, preferred_element_type=jnp.float32) + bias_up
    activated_full, gelu_pull = jax.vjp(exact_gelu, hidden_up)
    activated = activated_full.astype(jnp.bfloat16)
    branch = jnp.dot(activated, w_down, preferred_element_type=jnp.float32) + biases[4]
    out_full, second_pull = jax.vjp(layer_norm, norm_one + branch, norm_gains[1], biases[5])
    leading = out_full.reshape(own_seqs, SLOT, D)[:, 0].astype(jnp.bfloat16)
    pooled = jnp.tanh(jnp.dot(leading, w_pool, preferred_element_type=jnp.float32) + biases[6])
    pooled_low = pooled.astype(jnp.bfloat16)
    logits = against(pooled_low, w_class)
    onehot = (jnp.arange(CLASSES)[None, :] == own_labels[:, None]).astype(jnp.float32)
    losses = jax.nn.logsumexp(logits, axis=-1) - jnp.sum(onehot * logits, axis=-1)
    d_logits = jax.nn.softmax(logits, axis=-1) - onehot
    g_class = exact(d_logits.T, pooled_low.astype(jnp.float32))
    d_pre = exact(d_logits, w_class.astype(jnp.float32)) * (1.0 - pooled * pooled)
    g_pool = exact(leading.astype(jnp.float32).T, d_pre)
    g_pool_bias = jnp.sum(d_pre, axis=0)
    d_leading = exact(d_pre, w_pool.astype(jnp.float32).T)
    d_out = cotangent.astype(jnp.float32) * slot_live[:, None]
    d_out = d_out.reshape(own_seqs, SLOT, D).at[:, 0].add(d_leading).reshape(tok_rows, D)
    d_h2, g_gain_two, g_shift_two = second_pull(d_out)
    d_branch = d_h2.astype(jnp.bfloat16)
    g_bias_down = jnp.sum(d_branch.astype(jnp.float32), axis=0)
    g_down = inner(activated, d_branch)
    d_activated = against(d_branch, w_down)
    d_up = gelu_pull(d_activated)[0].astype(jnp.bfloat16)
    g_bias_up = jnp.sum(d_up.astype(jnp.float32), axis=0)
    g_up = inner(norm_low, d_up)
    d_norm_one = d_h2 + against(d_up, w_up)
    d_h1, g_gain_one, g_shift_one = first_pull(d_norm_one)
    d_attn = d_h1.astype(jnp.bfloat16)
    g_bias_out = jnp.sum(d_attn.astype(jnp.float32), axis=0)
    g_out = inner(context_tok, d_attn)
    d_context = against(d_attn, w_out).astype(jnp.bfloat16)
    d_context_heads = lax.all_to_all(
        d_context.reshape(tok_rows, head_parts, slice_width),
        "head",
        split_axis=1,
        concat_axis=0,
        tiled=True,
    )
    d_context_seq = d_context_heads.reshape(head_parts * own_seqs, SLOT, local_heads, HEAD_DIM)
    d_seq = lax.map(attend_backward, (seq_view, log_total, d_context_seq, lengths))
    d_back = lax.all_to_all(
        d_seq.reshape(head_parts * tok_rows, 3, 1, slice_width),
        "head",
        split_axis=0,
        concat_axis=2,
        tiled=True,
    )
    d_packed = d_back.reshape(tok_rows, 3 * D)
    g_qkv = inner(tokens, d_packed)
    column_sums = jnp.sum(d_packed.astype(jnp.float32), axis=0)
    grad_tokens = (d_h1 + against(d_packed, w_qkv)).astype(jnp.bfloat16)
    g_biases = jnp.stack(
        [column_sums[:D], column_sums[2 * D :], g_bias_out, g_shift_one, g_bias_down, g_shift_two]
    )
    g_gains = jnp.stack([g_gain_one, g_gain_two])
    g_qkv, g_out, g_up, g_down, g_pool, g_class, g_biases, g_gains, g_bias_up, g_pool_bias = (
        lax.psum_scatter(g_qkv, ("batch", "head"), scatter_dimension=1, tiled=True),
        lax.psum_scatter(g_out, ("batch", "head"), scatter_dimension=1, tiled=True),
        lax.psum_scatter(g_up, ("batch", "head"), scatter_dimension=1, tiled=True),
        lax.psum_scatter(g_down, ("batch", "head"), scatter_dimension=1, tiled=True),
        lax.psum_scatter(g_pool, ("batch", "head"), scatter_dimension=1, tiled=True),
        lax.psum_scatter(g_class, ("batch", "head"), scatter_dimension=1, tiled=True),
        lax.psum_scatter(g_biases, ("batch", "head"), scatter_dimension=1, tiled=True),
        lax.psum_scatter(g_gains, ("batch", "head"), scatter_dimension=1, tiled=True),
        lax.psum_scatter(g_bias_up, ("batch", "head"), scatter_dimension=0, tiled=True),
        lax.psum_scatter(g_pool_bias, ("batch", "head"), scatter_dimension=0, tiled=True),
    )
    return (
        out_full.astype(jnp.bfloat16),
        grad_tokens,
        losses,
        g_qkv,
        g_out,
        g_up,
        g_down,
        g_pool,
        g_class,
        g_biases,
        g_gains,
        g_bias_up,
        g_pool_bias,
    )


def solution(mesh):
    return jax.shard_map(
        per_device,
        mesh=mesh,
        in_specs=(
            P(("batch", "head"), None),
            P(("batch", "head"), None),
            P("batch"),
            P("batch"),
            P(),
            P(),
            P(),
            P(),
            P(),
            P(),
            P(),
            P(),
            P(),
        ),
        out_specs=(
            P(("batch", "head"), None),
            P(("batch", "head"), None),
            P(("batch", "head")),
            P(None, ("batch", "head")),
            P(None, ("batch", "head")),
            P(None, ("batch", "head")),
            P(None, ("batch", "head")),
            P(None, ("batch", "head")),
            P(None, ("batch", "head")),
            P(None, ("batch", "head")),
            P(None, ("batch", "head")),
            P(("batch", "head")),
            P(("batch", "head")),
        ),
        check_vma=False,
    )
```

profile of v0, /device:TPU:0, one launch (start us, length us, event | category | flops | bytes accessed | tf_op | source)
XLA Modules:
  0.0 791.8 jit_solution(17786111128805935081)
XLA Ops:
  7.2 1.6 slice_reduce_fusion.1
  9.3 4.5 fusion.34
  13.8 4.3 copy.63
  18.1 3.2 copy.64
  21.3 4.7 all-to-all-start
  26.0 29.1 %all-to-all-done = bf16[512,3,4,192]{0,3,1,2:T(8,128)(2,1)} async-done(((bf16[512,3,4,192]{0,3,1,2:T(8,128)(2,1)}), bf16[512,3,4,192]{0,3,1,2:T(8,128)(2,1)}, u32[]{:S(2)}, u32[]{:S(2)}) %all-to-all-start) | async-done | bytes 2359328 | tf_op jit(solution)/shard_map/all_to_all | solution.py:115
  55.1 24.0 %while.23 = (s32[]{:T(128)}, bf16[4,512,3,64]{1,3,2,0:T(8,128)(2,1)}, f32[4,3,512,1]{2,1,3,0:T(4,128)}, bf16[4,512,3,3,64]{1,4,3,2,0:T(8,128)(2,1)}, s32[4]{0:T(128)S(1)}, /*index=5*/s32[]{:T(128)}) while((s32[]{:T(128)}, bf16[4,512,3,64]{1,3,2,0:T(8,128)(2,1)}, f32[4,3,512,1]{2,1,3,0:T(4,128)}, bf16[4,512,3,3,64]{1,4,3,2,0:T(8,128)(2,1)}, ...), condition=%wide.region_3.4_spmd, body=%wide.region_0.3_spmd.sunk | while | flops 210074624 | bytes 11459673 | solution.py:123
  59.6 1.5 fusion.102
  65.6 1.5 fusion.102
  71.6 1.5 fusion.102
  77.6 1.5 fusion.102
  79.1 2.6 copy.65
  81.8 2.8 reshape.337
  85.1 3.0 reduce.38
  88.1 2.2 copy.87
  90.3 3.9 reshape.384
  94.3 4.2 all-to-all-start.1
  104.6 5.5 all-to-all-done.1
  110.2 4.1 reshape.385
  114.3 5.7 copy.67
  120.1 3.0 all_to_all.48
  124.4 2.7 fusion.56
  128.2 19.6 %multiply_convert_fusion.1 = (bf16[512,3072]{1,0:T(8,128)(2,1)S(1)}, f32[512,3072]{1,0:T(8,128)}, f32[512,3072]{1,0:T(8,128)}) fusion(f32[3072]{0:T(1024)S(1)} %copy-done.37, bf16[768,3072]{1,0:T(8,128)(2,1)} %param.25, f32[512,768]{1,0:T(8,128)S(1)} %get-tuple-element.165, f32[768]{0:T(1024)S(1)} %copy-done.32, f32[768]{0:T(1024)S(1)} %get-tuple-element.176, ...), kind=kOutput, calls=%fused_computation.50 | convolution fusion | flops 2521694208 | bytes 22042624 | tf_op jit(solution)/shard_map/dot_general | solution.py:136
  148.0 2.8 fusion.57
  155.5 2.0 fusion.45
  157.5 1.9 divide_subtract_fusion
  163.2 3.2 multiply_reduce_fusion.1
  167.2 2.1 fusion.53
  169.3 1.7 broadcast_multiply_fusion
  171.0 1.6 convert_reduce_fusion.2
  172.7 9.5 %convert_reduce_fusion = (f32[3072]{0:T(1024)}, bf16[512,3072]{1,0:T(8,128)(2,1)S(1)}) fusion(f32[512,3072]{1,0:T(8,128)} %get-tuple-element.156, f32[512,3072]{1,0:T(8,128)} %get-tuple-element.166, f32[3072]{0:T(1024)} %param.31, bf16[512,768]{1,0:T(8,128)(2,1)S(1)} %get-tuple-element.148, bf16[3072,768]{1,0:T(8,128)(2,1)} %param.26), kind=kOutput, calls=%fused_computation.48 | convolution fusion | flops 2442654720 | bytes 21258240 | tf_op jit(solution)/shard_map/dot_general | solution.py:30
  182.2 7.3 multiply_reduce_fusion.2
  192.4 1.7 convolution_convert_fusion
  194.1 2.3 copy.69
  196.5 4.2 all-to-all-start.2
  200.9 3.6 fusion.60
  204.6 7.8 all-to-all-done.2
  212.4 39.9 %while.24 = (s32[]{:T(128)}, bf16[4,512,3,3,64]{1,4,3,2,0:T(8,128)(2,1)}, bf16[4,512,3,3,64]{1,4,3,2,0:T(8,128)(2,1)}, s32[4]{0:T(128)}, f32[4,3,512,1]{2,1,3,0:...) while((s32[]{:T(128)}, bf16[4,512,3,3,64]{1,4,3,2,0:T(8,128)(2,1)}, ...), condition=%wide.region_16.17_spmd, body=%wide.region_14.16_spmd.sunk | while | flops 512654336 | bytes 27953856 | solution.py:177
  213.5 1.5 fusion.108
  219.9 1.6 fusion.109
  223.5 1.5 fusion.108
  230.0 1.5 fusion.109
  233.5 1.5 fusion.108
  239.9 1.6 fusion.109
  243.5 1.5 fusion.108
  249.9 1.5 fusion.109
  252.3 4.9 copy.70
  257.2 5.9 reshape.346
  263.1 7.0 copy.71
  270.0 53.9 %all_to_all.60 = bf16[2048,3,1,192]{3,1,2,0:T(4,128)(2,1)} all-to-all(bf16[2048,3,1,192]{3,1,2,0:T(4,128)(2,1)} %copy.71), channel_id=1, replica_groups=mesh['batch'=8,'head'=4] {'head'}, dimensions={0} | all-to-all | bytes 4718592 | tf_op jit(solution)/shard_map/all_to_all | solution.py:178
  323.9 7.4 copy.80
  331.3 2.2 copy.73
  333.6 1.4 copy-done.5
  335.0 5.0 convolution_bitcast_fusion
  340.2 8.8 %fusion.48 = f32[768,3072]{0,1:T(8,128)} fusion(bf16[512,3072]{1,0:T(8,128)(2,1)} %copy-done.43, f32[512,768]{1,0:T(8,128)} %copy-done.6, f32[768]{0:T(1024)} %get-tuple-element.107, f32[768]{0:T(1024)S(1)} %copy-done.27, f32[512]{0:T(512)} %copy-done.28, f32[512]{0:T(512)S(1)} %copy-done.17), kind=kOutput, calls=%fused_computation.138 | convolution fusion | flops 2417885184 | bytes 14166016 | tf_op jit(solution)/shard_map/dot_general | solution.py:24
  349.1 8.4 %fusion.61 = f32[3072,768]{0,1:T(8,128)} fusion(bf16[512,3072]{1,0:T(8,128)(2,1)} %copy-done.42, bf16[512,768]{1,0:T(8,128)(2,1)} %copy-done.13), kind=kOutput, calls=%fused_computation.148 | convolution fusion | flops 2415919104 | bytes 13369344 | tf_op jit(solution)/shard_map/dot_general | solution.py:24
  365.2 2.7 convert_reduce_fusion.1
  368.6 1.6 copy.74
  371.5 1.6 copy.75
  375.8 42.2 %all-reduce.5 = (f32[3,768]{1,0:T(4,128)}, f32[6,768]{1,0:T(8,128)}, f32[2,768]{1,0:T(2,128)}, f32[3072]{0:T(1024)}, f32[768]{0:T(1024)}) all-reduce(f32[3,768]{1,0:T(4,128)S(1)} %broadcast_multiply_fusion.1, f32[6,768]{1,0:T(8,128)} %stack.38, ...), channel_id=7, replica_groups=mesh['batch'=8,'head'=4] {'batch','head'}, use_global_device_ids=true, to_apply=%region_24.25.clone | all-reduce | flops 12288 | bytes 98304
  424.6 5.1 add_convert_fusion.1
  429.7 70.9 %reduce-scatter.9.cloned.1.call-done = f32[768,72]{0,1:T(8,128)} async-done(((f32[768,2304]{0,1:T(8,128)}), f32[768,72]{0,1:T(8,128)}) %reduce-scatter.9.cloned.1.call-update) | async-done | bytes 221200 | tf_op jit(solution)/shard_map/reduce_scatter | solution.py:194
  500.6 142.2 %reduce-scatter.13.cloned.1.call-done = f32[768,96]{0,1:T(8,128)} async-done(((f32[768,3072]{0,1:T(8,128)}), f32[768,96]{0,1:T(8,128)}) %reduce-scatter.13.cloned.1.call-update) | async-done | bytes 294928 | tf_op jit(solution)/shard_map/reduce_scatter | solution.py:196
  642.8 140.9 %reduce-scatter.15.cloned.1.call-done = f32[3072,24]{0,1:T(8,128)} async-done(((f32[3072,768]{0,1:T(8,128)}), f32[3072,24]{0,1:T(8,128)}) %reduce-scatter.15.cloned.1.call-update) | async-done | bytes 294928 | tf_op jit(solution)/shard_map/reduce_scatter | solution.py:197
  (222 shorter events, 83.8 us)
Async XLA Ops:
  7.2 2.1 copy-start
  8.8 139.0 %copy-start.26 = (f32[768]{0:T(1024)}, f32[768]{0:T(1024)S(1)}, u32[]{:S(2)}) copy-start(f32[768]{0:T(1024)S(1)} %get-tuple-element.176) | copy-start | bytes 9220
  21.3 33.8 %copy-start.40 = (s32[4]{0:T(128)S(1)}, s32[4]{0:T(128)}, u32[]{:S(2)}) copy-start(s32[4]{0:T(128)} %param.21) | copy-start | bytes 52
  21.3 33.8 %all-to-all-start = ((bf16[512,3,4,192]{0,3,1,2:T(8,128)(2,1)}), bf16[512,3,4,192]{0,3,1,2:T(8,128)(2,1)}, u32[]{:S(2)}, u32[]{:S(2)}) async-start(bf16[512,3,4,192]{0,3,1,2:T(8,128)(2,1)} %copy.64), calls=%async_computation | async-start | bytes 4718592 | tf_op jit(solution)/shard_map/all_to_all | solution.py:115
  85.1 15.2 %copy-start.39 = (s32[4]{0:T(128)S(1)}, s32[4]{0:T(128)}, u32[]{:S(2)}) copy-start(s32[4]{0:T(128)} %param.22) | copy-start | bytes 52
  94.3 15.9 %all-to-all-start.1 = ((bf16[4,2,49152]{2,1,0:T(2,128)(2,1)}), bf16[4,2,49152]{2,1,0:T(2,128)(2,1)}, u32[]{:S(2)}, u32[]{:S(2)}) async-start(bf16[4,2,49152]{2,1,0:T(2,128)(2,1)} %reshape.384), calls=%async_computation.1 | async-start | bytes 1572864 | tf_op jit(solution)/shard_map/all_to_all | solution.py:124
  98.5 331.2 %reduce-scatter.17.cloned.1.call-start = ((), (), s32[]{:S(2)}) async-start(), calls=%async_computation.13 | async-start | bytes 2433024 | tf_op jit(solution)/shard_map/reduce_scatter | solution.py:198
  102.9 1.1 copy-start.3
  114.3 10.0 %copy-start.34 = (f32[768]{0:T(1024)S(1)}, f32[768]{0:T(1024)}, u32[]{:S(2)}) copy-start(f32[768]{0:T(1024)} %get-tuple-element.108) | copy-start | bytes 9220
  124.3 3.1 copy-start.11
  124.3 3.9 copy-start.32
  124.3 3.9 copy-start.37
  124.4 23.6 %slice-start = ((s8[4718592]{0:T(1024)(128)(4,1)}), s8[4194304]{0:T(1024)(128)(4,1)S(1)}, s32[]{:S(2)}) async-start(s8[4718592]{0:T(1024)(128)(4,1)} %bitcast.202), calls=%async_computation.14 | async-start | bytes 8388608
  127.1 20.8 %copy-start.6 = (f32[512,768]{1,0:T(8,128)}, f32[512,768]{1,0:T(8,128)S(1)}, u32[]{:S(2)}) copy-start(f32[512,768]{1,0:T(8,128)S(1)} %get-tuple-element.165) | copy-start | bytes 4718596
  127.1 20.8 %copy-start.16 = (f32[512]{0:T(512)}, f32[512]{0:T(512)S(1)}, u32[]{:S(2)}) copy-start(f32[512]{0:T(512)S(1)} %broadcast_multiply_fusion.3) | copy-start | bytes 6148
  127.4 0.8 copy-start.18
  128.2 19.7 %copy-start.28 = (f32[512]{0:T(512)}, f32[512]{0:T(512)S(1)}, u32[]{:S(2)}) copy-start(f32[512]{0:T(512)S(1)} %fusion.43) | copy-start | bytes 6148
  128.2 19.7 %copy-start.33 = (f32[768]{0:T(1024)S(1)}, f32[768]{0:T(1024)}, u32[]{:S(2)}) copy-start(f32[768]{0:T(1024)} %get-tuple-element.106) | copy-start | bytes 9220
  128.2 19.7 %slice-start.1 = ((s8[4718592]{0:T(1024)(128)(4,1)}), s8[524288]{0:T(1024)(128)(4,1)S(1)}, s32[]{:S(2)}) async-start(s8[4718592]{0:T(1024)(128)(4,1)} %bitcast.202), calls=%async_computation.15 | async-start | bytes 1048576
  147.9 2.9 copy-start.42
  150.7 10.5 %copy-start.1 = (f32[512,768]{1,0:T(8,128)}, f32[512,768]{1,0:T(8,128)S(1)}, u32[]{:S(2)}) copy-start(f32[512,768]{1,0:T(8,128)S(1)} %get-tuple-element.168) | copy-start | bytes 4718596
  150.8 1.9 copy-start.10
  150.8 1.9 copy-start.15
  150.8 2.7 copy-start.38
  150.8 10.5 %copy-start.25 = (f32[768]{0:T(1024)S(1)}, f32[768]{0:T(1024)}, u32[]{:S(2)}) copy-start(f32[768]{0:T(1024)} %slice_reduce_fusion) | copy-start | bytes 9220
  151.1 0.6 copy-start.20
  159.4 1.9 copy-start.35
  163.2 3.9 copy-start.2
  163.2 3.9 copy-start.4
  166.5 2.8 copy-start.30
  166.5 2.8 copy-start.23
  172.6 9.6 %copy-start.13 = (bf16[512,768]{1,0:T(8,128)(2,1)}, bf16[512,768]{1,0:T(8,128)(2,1)S(1)}, u32[]{:S(2)}) copy-start(bf16[512,768]{1,0:T(8,128)(2,1)S(1)} %get-tuple-element.148) | copy-start | bytes 2359300
  172.6 9.6 %copy-start.7 = (f32[512,768]{1,0:T(8,128)S(1)}, f32[512,768]{1,0:T(8,128)}, u32[]{:S(2)}) copy-start(f32[512,768]{1,0:T(8,128)} %copy-done.6) | copy-start | bytes 4718596
  172.6 9.6 %copy-start.9 = (f32[512,768]{1,0:T(8,128)S(1)}, f32[512,768]{1,0:T(8,128)}, u32[]{:S(2)}) copy-start(f32[512,768]{1,0:T(8,128)} %get-tuple-element.154) | copy-start | bytes 4718596
  172.7 9.6 %copy-start.17 = (f32[512]{0:T(512)S(1)}, f32[512]{0:T(512)}, u32[]{:S(2)}) copy-start(f32[512]{0:T(512)} %copy-done.16) | copy-start | bytes 6148
  172.7 9.5 %copy-start.27 = (f32[768]{0:T(1024)S(1)}, f32[768]{0:T(1024)}, u32[]{:S(2)}) copy-start(f32[768]{0:T(1024)} %copy-done.26) | copy-start | bytes 9220
  172.7 9.5 %copy-start.29 = (f32[512]{0:T(512)S(1)}, f32[512]{0:T(512)}, u32[]{:S(2)}) copy-start(f32[512]{0:T(512)} %copy-done.28) | copy-start | bytes 6148
  182.2 7.3 copy-start.43
  182.2 7.3 copy-start.19
  189.5 2.9 copy-start.36
  190.2 1.2 copy-start.8
  190.2 1.4 copy-start.31
  191.6 0.9 copy-start.12
  196.5 15.9 %all-to-all-start.2 = ((bf16[512,4,192]{0,2,1:T(8,128)(2,1)}), bf16[512,4,192]{0,2,1:T(8,128)(2,1)}, u32[]{:S(2)}, u32[]{:S(2)}) async-start(bf16[512,4,192]{0,2,1:T(8,128)(2,1)} %bitcast.198), calls=%async_computation.2 | async-start | bytes 1572864 | tf_op jit(solution)/shard_map/all_to_all | solution.py:169
  200.7 229.0 %reduce-scatter.11.cloned.1.call-start = ((), (), s32[]{:S(2)}) async-start(), calls=%async_computation.10 | async-start | bytes 2433024 | tf_op jit(solution)/shard_map/reduce_scatter | solution.py:195
  204.6 296.0 %reduce-scatter.9.cloned.1.call-start = ((), (), s32[]{:S(2)}) async-start(), calls=%async_computation.9 | async-start | bytes 7299072 | tf_op jit(solution)/shard_map/reduce_scatter | solution.py:194
  212.4 3.4 copy-start.41
  222.4 3.4 copy-start.41
  232.3 3.4 copy-start.41
  242.4 3.4 copy-start.41
  331.3 3.6 copy-start.14
  333.6 1.4 copy-start.5
  339.9 302.9 %reduce-scatter.13.cloned.1.call-start = ((), (), s32[]{:S(2)}) async-start(), calls=%async_computation.11 | async-start | bytes 9732096 | tf_op jit(solution)/shard_map/reduce_scatter | solution.py:196
  349.1 434.6 %reduce-scatter.15.cloned.1.call-start = ((), (), s32[]{:S(2)}) async-start(), calls=%async_computation.12 | async-start | bytes 9732096 | tf_op jit(solution)/shard_map/reduce_scatter | solution.py:197
  357.5 2.5 copy-start.22
  357.5 3.8 copy-start.21
  358.2 17.6 %copy-start.24 = (f32[768]{0:T(1024)S(1)}, f32[768]{0:T(1024)}, u32[]{:S(2)}) copy-start(f32[768]{0:T(1024)} %get-tuple-element.172) | copy-start | bytes 9220
Sparse Core Ops, SparseCore 0:
  171.1 100.1 reduce-scatter.16
  278.1 98.0 reduce-scatter.10
  382.4 118.0 reduce-scatter.8
  507.9 134.8 reduce-scatter.12
  649.1 134.5 reduce-scatter.14
where the time goes:
time: 800 us; the launch traced here: 792 us
  waiting for transfers between devices  397 us (50%)
  matrix products  112 us (14%)
  local copies, waits for them, and re-layouts  111 us (14%)
  blocking collectives  96.1 us (12%)
  other arithmetic  42.7 us (5%)
  between operations  18.5 us (2%)
  starting transfers between devices  14.2 us (2%)
    reduce_scatter x1, waiting for transfers between devices, per_device(): lax.psum_scatter(g_up, ('batch', 'head'), scatter_dimension=1, tiled=True)  142 us
    reduce_scatter x1, waiting for transfers between devices, per_device(): lax.psum_scatter(g_down, ('batch', 'head'), scatter_dimension=1, tiled=True)  141 us
    reduce_scatter x1, waiting for transfers between devices, per_device(): lax.psum_scatter(g_qkv, ('batch', 'head'), scatter_dimension=1, tiled=True)  70.9 us
    all_to_all x1, blocking collectives, per_device(): lax.all_to_all(d_seq.reshape(head_parts * tok_rows, 3, 1, slice_width), '...  53.9 us
    unnamed x1, blocking collectives  42.2 us
    all_to_all x1, waiting for transfers between devices, per_device(): lax.all_to_all(packed_low.reshape(tok_rows, 3, head_parts, slice_width),...  29.1 us
    dot_general x4, matrix products, inner(): lax.dot_general(left, right, (((0,), (0,)), ((), ())), preferred_element_...  25.8 us
    dot_general x5, matrix products, against(): lax.dot_general(left, right, (((1,), (1,)), ((), ())), preferred_element_...  24.3 us
  transfers between devices with their start and end apart: 8, of which 6 were waited for; matrix products, arithmetic and copies ran while one was open for 19% of the time, Pallas kernels for 0%

commit v1 on v0

--- a/solution.py
+++ b/solution.py
@@ -121,13 +121,12 @@
     )
     seq_view = head_view.reshape(head_parts * own_seqs, SLOT, 3, local_heads, HEAD_DIM)
     context, log_total = lax.map(attend_forward, (seq_view, lengths))
-    context_back = lax.all_to_all(
-        context.reshape(head_parts * tok_rows, 1, slice_width),
-        "head",
-        split_axis=0,
-        concat_axis=1,
-        tiled=True,
-    )
+    a0 = context.reshape(head_parts * tok_rows, 1, slice_width)
+    long_array = lax.psum(1, "head")
+    wide_out = jnp.split(a0, long_array, axis=0)
+    z1 = jnp.stack(wide_out)
+    block_out = lax.all_to_all(z1, "head", 0, 0)
+    context_back = jnp.concatenate(block_out, axis=1)
     context_tok = context_back.reshape(tok_rows, D)
     attn = jnp.dot(context_tok, w_out, preferred_element_type=jnp.float32) + biases[2]
     first_sum = tokens.astype(jnp.float32) + attn

time: 800 us -> 773 us (0.966)
  local copies, waits for them, and re-layouts: 111 us -> 86.1 us
    unnamed x98 -> x91, local copies, waits for them, and re-layouts: 23.3 us -> 13 us
    all_to_all x3 -> x0, local copies, waits for them, and re-layouts: 9.99 us -> none  [per_device(): lax.all_to_all(context.reshape(head_parts * tok_rows, 1, slice_width), 'h...]
  transfers between devices with their start and end apart: 8 -> 8, of which waited for: 6 -> 6; matrix products, arithmetic and copies ran while one was open for 19% -> 20% of each run, Pallas kernels for 0% -> 0%
where the time goes in v1:
time: 773 us; the launch traced here: 765 us
  waiting for transfers between devices  397 us (51%)
  matrix products  113 us (15%)
  blocking collectives  96.7 us (13%)
  local copies, waits for them, and re-layouts  86.1 us (11%)
  other arithmetic  40.6 us (5%)
  between operations  18.3 us (2%)
  starting transfers between devices  13.2 us (2%)
    reduce_scatter x1, waiting for transfers between devices, per_device(): lax.psum_scatter(g_up, ('batch', 'head'), scatter_dimension=1, tiled=True)  142 us
    reduce_scatter x1, waiting for transfers between devices, per_device(): lax.psum_scatter(g_down, ('batch', 'head'), scatter_dimension=1, tiled=True)  141 us
    reduce_scatter x1, waiting for transfers between devices, per_device(): lax.psum_scatter(g_qkv, ('batch', 'head'), scatter_dimension=1, tiled=True)  70.7 us
    all_to_all x1, blocking collectives, per_device(): lax.all_to_all(d_seq.reshape(head_parts * tok_rows, 3, 1, slice_width), '...  54.1 us
    unnamed x1, blocking collectives  42.6 us
    all_to_all x1, waiting for transfers between devices, per_device(): lax.all_to_all(packed_low.reshape(tok_rows, 3, head_parts, slice_width),...  29.1 us
    dot_general x4, matrix products, inner(): lax.dot_general(left, right, (((0,), (0,)), ((), ())), preferred_element_...  25.8 us
    dot_general x5, matrix products, against(): lax.dot_general(left, right, (((1,), (1,)), ((), ())), preferred_element_...  24.4 us
  transfers between devices with their start and end apart: 8, of which 6 were waited for; matrix products, arithmetic and copies ran while one was open for 20% of the time, Pallas kernels for 0%

profile of v1, /device:TPU:0, one launch (start us, length us, event | category | flops | bytes accessed | tf_op | source)
XLA Modules:
  0.0 765.3 jit_solution(544937717018692600)
XLA Ops:
  7.2 1.6 slice_reduce_fusion.1
  9.3 4.5 fusion.34
  13.8 4.3 copy.57
  18.1 3.2 copy.58
  21.3 4.7 all-to-all-start
  26.0 29.1 %all-to-all-done = bf16[512,3,4,192]{0,3,1,2:T(8,128)(2,1)} async-done(((bf16[512,3,4,192]{0,3,1,2:T(8,128)(2,1)}), bf16[512,3,4,192]{0,3,1,2:T(8,128)(2,1)}, u32[]{:S(2)}, u32[]{:S(2)}) %all-to-all-start) | async-done | bytes 2359328 | tf_op jit(solution)/shard_map/all_to_all | solution.py:115
  55.1 24.0 %while.23 = (s32[]{:T(128)}, bf16[4,512,3,64]{1,3,2,0:T(8,128)(2,1)}, f32[4,3,512,1]{2,1,3,0:T(4,128)}, bf16[4,512,3,3,64]{1,4,3,2,0:T(8,128)(2,1)}, s32[4]{0:T(128)S(1)}, /*index=5*/s32[]{:T(128)}) while((s32[]{:T(128)}, bf16[4,512,3,64]{1,3,2,0:T(8,128)(2,1)}, f32[4,3,512,1]{2,1,3,0:T(4,128)}, bf16[4,512,3,3,64]{1,4,3,2,0:T(8,128)(2,1)}, ...), condition=%wide.region_3.4_spmd, body=%wide.region_0.3_spmd.sunk | while | flops 210074624 | bytes 11459673 | solution.py:123
  59.6 1.5 fusion.103
  65.6 1.5 fusion.103
  71.6 1.5 fusion.103
  77.6 1.5 fusion.103
  81.4 4.2 all-to-all-start.1
  88.1 1.4 convert_multiply_fusion
  91.3 6.1 all-to-all-done.1
  97.3 2.8 fusion.57
  101.3 20.0 %multiply_convert_fusion.1 = (bf16[512,3072]{1,0:T(8,128)(2,1)S(1)}, f32[512,3072]{1,0:T(8,128)}, f32[512,3072]{1,0:T(8,128)}) fusion(f32[3072]{0:T(1024)S(1)} %copy-done.35, bf16[768,3072]{1,0:T(8,128)(2,1)} %param.25, f32[512,768]{1,0:T(8,128)S(1)} %get-tuple-element.169, f32[768]{0:T(1024)S(1)} %copy-done.31, f32[768]{0:T(1024)S(1)} %get-tuple-element.180, ...), kind=kOutput, calls=%fused_computation.50 | convolution fusion | flops 2521694208 | bytes 22042624 | tf_op jit(solution)/shard_map/dot_general | solution.py:135
  121.3 2.8 fusion.58
  128.9 2.0 fusion.45
  130.9 1.9 divide_subtract_fusion
  135.3 1.4 scatter-add.4
  136.6 3.2 multiply_reduce_fusion.1
  140.6 2.1 fusion.53
  142.7 1.7 broadcast_multiply_fusion
  144.4 1.6 convert_reduce_fusion.2
  146.1 9.7 %convert_reduce_fusion = (f32[3072]{0:T(1024)}, bf16[512,3072]{1,0:T(8,128)(2,1)S(1)}) fusion(f32[512,3072]{1,0:T(8,128)} %get-tuple-element.156, f32[512,3072]{1,0:T(8,128)} %get-tuple-element.170, f32[3072]{0:T(1024)} %param.31, bf16[512,768]{1,0:T(8,128)(2,1)S(1)} %get-tuple-element.148, bf16[3072,768]{1,0:T(8,128)(2,1)} %param.26), kind=kOutput, calls=%fused_computation.48 | convolution fusion | flops 2442654720 | bytes 21258240 | tf_op jit(solution)/shard_map/dot_general | solution.py:30
  155.8 7.3 multiply_reduce_fusion.2
  166.0 1.7 convolution_convert_fusion
  167.7 2.3 copy.59
  170.0 4.2 all-to-all-start.2
  174.3 3.6 fusion.61
  177.9 8.0 %all-to-all-done.2 = bf16[512,4,192]{0,2,1:T(8,128)(2,1)} async-done(((bf16[512,4,192]{0,2,1:T(8,128)(2,1)}), bf16[512,4,192]{0,2,1:T(8,128)(2,1)}, u32[]{:S(2)}, u32[]{:S(2)}) %all-to-all-start.2) | async-done | bytes 786464 | tf_op jit(solution)/shard_map/all_to_all | solution.py:168
  185.9 39.9 %while.24 = (s32[]{:T(128)}, bf16[4,512,3,3,64]{1,4,3,2,0:T(8,128)(2,1)}, bf16[4,512,3,3,64]{1,4,3,2,0:T(8,128)(2,1)}, s32[4]{0:T(128)}, f32[4,3,512,1]{2,1,3,0:...) while((s32[]{:T(128)}, bf16[4,512,3,3,64]{1,4,3,2,0:T(8,128)(2,1)}, ...), condition=%wide.region_16.17_spmd, body=%wide.region_14.16_spmd.sunk | while | flops 512654336 | bytes 27953856 | solution.py:176
  187.0 1.5 fusion.109
  193.5 1.6 fusion.110
  197.0 1.5 fusion.109
  203.5 1.5 fusion.110
  207.0 1.5 fusion.109
  213.4 1.6 fusion.110
  217.0 1.5 fusion.109
  223.4 1.5 fusion.110
  225.8 4.9 copy.60
  230.7 5.9 reshape.350
  236.6 7.0 copy.61
  243.6 54.1 %all_to_all.50 = bf16[2048,3,1,192]{3,1,2,0:T(4,128)(2,1)} all-to-all(bf16[2048,3,1,192]{3,1,2,0:T(4,128)(2,1)} %copy.61), channel_id=1, replica_groups=mesh['batch'=8,'head'=4] {'head'}, dimensions={0} | all-to-all | bytes 4718592 | tf_op jit(solution)/shard_map/all_to_all | solution.py:177
  297.6 7.4 copy.70
  305.0 2.2 copy.63
  307.3 1.4 copy-done.5
  308.7 5.0 convolution_bitcast_fusion
  313.7 8.8 %fusion.48 = f32[768,3072]{0,1:T(8,128)} fusion(bf16[512,3072]{1,0:T(8,128)(2,1)} %copy-done.41, f32[512,768]{1,0:T(8,128)} %copy-done.6, f32[768]{0:T(1024)} %get-tuple-element.107, f32[768]{0:T(1024)S(1)} %copy-done.26, f32[512]{0:T(512)} %copy-done.27, f32[512]{0:T(512)S(1)} %copy-done.16), kind=kOutput, calls=%fused_computation.139 | convolution fusion | flops 2417885184 | bytes 14166016 | tf_op jit(solution)/shard_map/dot_general | solution.py:24
  322.6 8.4 %fusion.62 = f32[3072,768]{0,1:T(8,128)} fusion(bf16[512,3072]{1,0:T(8,128)(2,1)} %copy-done.40, bf16[512,768]{1,0:T(8,128)(2,1)} %copy-done.12), kind=kOutput, calls=%fused_computation.150 | convolution fusion | flops 2415919104 | bytes 13369344 | tf_op jit(solution)/shard_map/dot_general | solution.py:24
  338.6 2.7 convert_reduce_fusion.1
  342.0 1.6 copy.64
  343.6 1.4 stack.54
  345.0 1.6 copy.65
  346.5 1.3 stack.55
  347.9 1.4 stack.58
  349.2 42.6 %all-reduce.5 = (f32[3,768]{1,0:T(4,128)}, f32[6,768]{1,0:T(8,128)}, f32[2,768]{1,0:T(2,128)}, f32[3072]{0:T(1024)}, f32[768]{0:T(1024)}) all-reduce(f32[3,768]{1,0:T(4,128)S(1)} %broadcast_multiply_fusion.1, f32[6,768]{1,0:T(8,128)} %stack.58, ...), channel_id=7, replica_groups=mesh['batch'=8,'head'=4] {'batch','head'}, use_global_device_ids=true, to_apply=%region_24.25.clone | all-reduce | flops 12288 | bytes 98304
  394.4 1.3 constant_dynamic-slice_fusion
  395.7 1.3 constant_dynamic-slice_fusion.2
  397.0 1.4 constant_dynamic-slice_fusion.1
  398.4 5.1 add_convert_fusion.1
  403.5 70.7 %reduce-scatter.9.cloned.1.call-done = f32[768,72]{0,1:T(8,128)} async-done(((f32[768,2304]{0,1:T(8,128)}), f32[768,72]{0,1:T(8,128)}) %reduce-scatter.9.cloned.1.call-update) | async-done | bytes 221200 | tf_op jit(solution)/shard_map/reduce_scatter | solution.py:193
  474.2 142.0 %reduce-scatter.13.cloned.1.call-done = f32[768,96]{0,1:T(8,128)} async-done(((f32[768,3072]{0,1:T(8,128)}), f32[768,96]{0,1:T(8,128)}) %reduce-scatter.13.cloned.1.call-update) | async-done | bytes 294928 | tf_op jit(solution)/shard_map/reduce_scatter | solution.py:195
  616.2 141.1 %reduce-scatter.15.cloned.1.call-done = f32[3072,24]{0,1:T(8,128)} async-done(((f32[3072,768]{0,1:T(8,128)}), f32[3072,24]{0,1:T(8,128)}) %reduce-scatter.15.cloned.1.call-update) | async-done | bytes 294928 | tf_op jit(solution)/shard_map/reduce_scatter | solution.py:196
  (210 shorter events, 72.6 us)
Async XLA Ops:
  7.2 2.1 copy-start
  8.8 112.4 %copy-start.25 = (f32[768]{0:T(1024)}, f32[768]{0:T(1024)S(1)}, u32[]{:S(2)}) copy-start(f32[768]{0:T(1024)S(1)} %get-tuple-element.180) | copy-start | bytes 9220
  21.3 33.8 %copy-start.38 = (s32[4]{0:T(128)S(1)}, s32[4]{0:T(128)}, u32[]{:S(2)}) copy-start(s32[4]{0:T(128)} %param.21) | copy-start | bytes 52
  21.3 33.8 %all-to-all-start = ((bf16[512,3,4,192]{0,3,1,2:T(8,128)(2,1)}), bf16[512,3,4,192]{0,3,1,2:T(8,128)(2,1)}, u32[]{:S(2)}, u32[]{:S(2)}) async-start(bf16[512,3,4,192]{0,3,1,2:T(8,128)(2,1)} %copy.58), calls=%async_computation | async-start | bytes 4718592 | tf_op jit(solution)/shard_map/all_to_all | solution.py:115
  79.1 7.8 %copy-start.37 = (s32[4]{0:T(128)S(1)}, s32[4]{0:T(128)}, u32[]{:S(2)}) copy-start(s32[4]{0:T(128)} %param.22) | copy-start | bytes 52
  81.4 15.9 %all-to-all-start.1 = ((bf16[4,512,1,192]{1,3,2,0:T(8,128)(2,1)}), bf16[4,512,1,192]{1,3,2,0:T(8,128)(2,1)}, u32[]{:S(2)}, u32[]{:S(2)}) async-start(bf16[4,512,1,192]{1,3,2,0:T(8,128)(2,1)} %pad_maximum_fusion), calls=%async_computation.1 | async-start | bytes 1572864 | tf_op jit(solution)/shard_map/all_to_all | solution.py:128
  85.6 317.9 %reduce-scatter.17.cloned.1.call-start = ((), (), s32[]{:S(2)}) async-start(), calls=%async_computation.13 | async-start | bytes 2433024 | tf_op jit(solution)/shard_map/reduce_scatter | solution.py:197
  89.5 1.1 copy-start.3
  97.3 3.9 copy-start.31
  97.3 3.9 copy-start.35
  97.3 24.0 %slice-start = ((s8[4718592]{0:T(1024)(128)(4,1)}), s8[4194304]{0:T(1024)(128)(4,1)S(1)}, s32[]{:S(2)}) async-start(s8[4718592]{0:T(1024)(128)(4,1)} %bitcast.204), calls=%async_computation.14 | async-start | bytes 8388608
  100.2 21.1 %copy-start.6 = (f32[512,768]{1,0:T(8,128)}, f32[512,768]{1,0:T(8,128)S(1)}, u32[]{:S(2)}) copy-start(f32[512,768]{1,0:T(8,128)S(1)} %get-tuple-element.169) | copy-start | bytes 4718596
  100.2 21.1 %copy-start.15 = (f32[512]{0:T(512)}, f32[512]{0:T(512)S(1)}, u32[]{:S(2)}) copy-start(f32[512]{0:T(512)S(1)} %broadcast_multiply_fusion.3) | copy-start | bytes 6148
  100.5 0.8 copy-start.17
  101.3 20.0 %copy-start.27 = (f32[512]{0:T(512)}, f32[512]{0:T(512)S(1)}, u32[]{:S(2)}) copy-start(f32[512]{0:T(512)S(1)} %fusion.43) | copy-start | bytes 6148
  101.3 20.0 %copy-start.32 = (f32[768]{0:T(1024)S(1)}, f32[768]{0:T(1024)}, u32[]{:S(2)}) copy-start(f32[768]{0:T(1024)} %get-tuple-element.106) | copy-start | bytes 9220
  101.3 20.0 %slice-start.1 = ((s8[4718592]{0:T(1024)(128)(4,1)}), s8[524288]{0:T(1024)(128)(4,1)S(1)}, s32[]{:S(2)}) async-start(s8[4718592]{0:T(1024)(128)(4,1)} %bitcast.204), calls=%async_computation.15 | async-start | bytes 1048576
  121.3 2.9 copy-start.40
  124.1 10.5 %copy-start.1 = (f32[512,768]{1,0:T(8,128)}, f32[512,768]{1,0:T(8,128)S(1)}, u32[]{:S(2)}) copy-start(f32[512,768]{1,0:T(8,128)S(1)} %get-tuple-element.172) | copy-start | bytes 4718596
  124.2 1.9 copy-start.10
  124.2 1.9 copy-start.14
  124.2 2.7 copy-start.36
  124.2 10.5 %copy-start.24 = (f32[768]{0:T(1024)S(1)}, f32[768]{0:T(1024)}, u32[]{:S(2)}) copy-start(f32[768]{0:T(1024)} %slice_reduce_fusion) | copy-start | bytes 9220
  124.5 0.6 copy-start.19
  132.8 1.9 copy-start.33
  136.6 3.9 copy-start.2
  136.6 3.9 copy-start.4
  139.9 2.8 copy-start.29
  139.9 2.8 copy-start.22
  146.0 9.7 %copy-start.12 = (bf16[512,768]{1,0:T(8,128)(2,1)}, bf16[512,768]{1,0:T(8,128)(2,1)S(1)}, u32[]{:S(2)}) copy-start(bf16[512,768]{1,0:T(8,128)(2,1)S(1)} %get-tuple-element.148) | copy-start | bytes 2359300
  146.0 9.7 %copy-start.7 = (f32[512,768]{1,0:T(8,128)S(1)}, f32[512,768]{1,0:T(8,128)}, u32[]{:S(2)}) copy-start(f32[512,768]{1,0:T(8,128)} %copy-done.6) | copy-start | bytes 4718596
  146.0 9.7 %copy-start.9 = (f32[512,768]{1,0:T(8,128)S(1)}, f32[512,768]{1,0:T(8,128)}, u32[]{:S(2)}) copy-start(f32[512,768]{1,0:T(8,128)} %get-tuple-element.154) | copy-start | bytes 4718596
  146.1 9.7 %copy-start.16 = (f32[512]{0:T(512)S(1)}, f32[512]{0:T(512)}, u32[]{:S(2)}) copy-start(f32[512]{0:T(512)} %copy-done.15) | copy-start | bytes 6148
  146.1 9.7 %copy-start.26 = (f32[768]{0:T(1024)S(1)}, f32[768]{0:T(1024)}, u32[]{:S(2)}) copy-start(f32[768]{0:T(1024)} %copy-done.25) | copy-start | bytes 9220
  146.1 9.7 %copy-start.28 = (f32[512]{0:T(512)S(1)}, f32[512]{0:T(512)}, u32[]{:S(2)}) copy-start(f32[512]{0:T(512)} %copy-done.27) | copy-start | bytes 6148
  155.8 7.3 copy-start.41
  155.8 7.3 copy-start.18
  163.1 2.9 copy-start.34
  163.7 1.2 copy-start.8
  163.8 1.4 copy-start.30
  165.1 0.9 copy-start.11
  170.0 15.9 %all-to-all-start.2 = ((bf16[512,4,192]{0,2,1:T(8,128)(2,1)}), bf16[512,4,192]{0,2,1:T(8,128)(2,1)}, u32[]{:S(2)}, u32[]{:S(2)}) async-start(bf16[512,4,192]{0,2,1:T(8,128)(2,1)} %bitcast.199), calls=%async_computation.2 | async-start | bytes 1572864 | tf_op jit(solution)/shard_map/all_to_all | solution.py:168
  174.2 229.3 %reduce-scatter.11.cloned.1.call-start = ((), (), s32[]{:S(2)}) async-start(), calls=%async_computation.10 | async-start | bytes 2433024 | tf_op jit(solution)/shard_map/reduce_scatter | solution.py:194
  177.9 296.3 %reduce-scatter.9.cloned.1.call-start = ((), (), s32[]{:S(2)}) async-start(), calls=%async_computation.9 | async-start | bytes 7299072 | tf_op jit(solution)/shard_map/reduce_scatter | solution.py:193
  185.9 3.4 copy-start.39
  195.9 3.4 copy-start.39
  205.8 3.4 copy-start.39
  215.9 3.4 copy-start.39
  305.0 3.6 copy-start.13
  307.3 1.4 copy-start.5
  313.7 302.5 %reduce-scatter.13.cloned.1.call-start = ((), (), s32[]{:S(2)}) async-start(), calls=%async_computation.11 | async-start | bytes 9732096 | tf_op jit(solution)/shard_map/reduce_scatter | solution.py:195
  322.5 434.8 %reduce-scatter.15.cloned.1.call-start = ((), (), s32[]{:S(2)}) async-start(), calls=%async_computation.12 | async-start | bytes 9732096 | tf_op jit(solution)/shard_map/reduce_scatter | solution.py:196
  331.0 2.5 copy-start.21
  331.0 3.8 copy-start.20
  331.6 17.6 %copy-start.23 = (f32[768]{0:T(1024)S(1)}, f32[768]{0:T(1024)}, u32[]{:S(2)}) copy-start(f32[768]{0:T(1024)} %get-tuple-element.176) | copy-start | bytes 9220
Sparse Core Ops, SparseCore 0:
  144.5 100.3 reduce-scatter.16
  251.7 98.0 reduce-scatter.10
  356.0 118.0 reduce-scatter.8
  481.5 134.6 reduce-scatter.12
  622.5 134.7 reduce-scatter.14
